TPU v7x, 32 devices: a whole 2x2x4 slice. The times are simulated.
32 devices in a mesh: gossip: 4 (over z), fsdp: 2 (over y), tensor: 4 (over x, core).
Axes of the slice: x: 2, y: 2, z: 4, core: 2. Of those that a mesh axis runs over, the one named last changes fastest.
Arguments:
- hidden: bfloat16 [4, 4, 256, 4096], P('gossip', 'fsdp', None, 'tensor'), may hold values from -6 to 6
- cotangent: bfloat16 [4, 4, 256, 4096], P('gossip', 'fsdp', None, 'tensor'), may hold values from -6 to 6
- documents: int32 [4, 4, 256], P('gossip', 'fsdp'), may hold values from 0 to 7, never falling along the last dimension, each value on 1 to 128 neighbouring positions
- q_weight: float32 [4, 4096, 2048], P('gossip', 'fsdp', 'tensor'), may hold values from -0.09375 to 0.09375
- k_weight: float32 [4, 4096, 512], P('gossip', 'fsdp', 'tensor'), may hold values from -0.09375 to 0.09375
- v_weight: float32 [4, 4096, 512], P('gossip', 'fsdp', 'tensor'), may hold values from -0.09375 to 0.09375
- o_weight: float32 [4, 4096, 2048], P('gossip', 'fsdp', 'tensor'), may hold values from -0.125 to 0.125
- edge_weight: float32 [4], P('gossip'), may hold values from 0.1 to 0.45
Outputs:
- new_q_weight: float32 [4, 4096, 2048], P('gossip', 'fsdp', 'tensor')
- new_k_weight: float32 [4, 4096, 512], P('gossip', 'fsdp', 'tensor')
- new_v_weight: float32 [4, 4096, 512], P('gossip', 'fsdp', 'tensor')
- new_o_weight: float32 [4, 4096, 2048], P('gossip', 'fsdp', 'tensor')
Inputs may be any that keep to these rules, and one draw needn't show every extreme that they name: `documents`: document ids never fall along a sequence; each document spans 1 to 128 positions, and some document spans exactly 128.
All inputs are finite; a program needn't handle non-finite values.
Results may differ from a plain program's by a relative error of at most 0.007.
Values may be sent and summed in bfloat16 or wider, within the bound.
No kernel may reach another device: no remote copies, remote signals or barrier semaphores. Data moves between devices by JAX's collectives and lax.ppermute only.
A program may use at most 128 MiB of HBM per device.

v0:
```python
import math
import jax
import jax.numpy as jnp
from jax import lax
from jax.sharding import PartitionSpec as P

HD = 128
rope_theta = 500000.0
learn_rate = 0.001
norm_eps = 1e-05


def passed_along(shard, axis, by):
    count = lax.axis_size(axis)
    return lax.ppermute(shard, axis, [(i, (i + by) % count) for i in range(count)])


def contract(form, left, right):
    return jnp.einsum(form, left, right, preferred_element_type=jnp.float32)


def rope_tables(length, head_size):
    half_dim = head_size // 2
    positions = jnp.arange(length, dtype=jnp.float32)
    freqs = jnp.exp(
        jnp.arange(half_dim, dtype=jnp.float32) * (-2.0 / head_size * math.log(rope_theta))
    )
    angles = positions[:, None] * freqs[None, :]
    return (jnp.cos(angles), jnp.sin(angles))


def rotate(values, cosine, sine_table):
    half_dim = values.shape[-1] // 2
    first_half = values[..., :half_dim]
    second_half = values[..., half_dim:]
    return jnp.concatenate(
        [
            first_half * cosine - second_half * sine_table,
            second_half * cosine + first_half * sine_table,
        ],
        -1,
    )


def unrotate(values, cosine, sine_table):
    half_dim = values.shape[-1] // 2
    first_half = values[..., :half_dim]
    second_half = values[..., half_dim:]
    return jnp.concatenate(
        [
            first_half * cosine + second_half * sine_table,
            second_half * cosine - first_half * sine_table,
        ],
        -1,
    )


def attention_grads(proj, d_ctx, documents, heads_q, heads_k):
    seq_count, length = documents.shape
    group_size = heads_q // heads_k
    q_cols = heads_q * HD
    kv_cols = heads_k * HD
    cosine, sine_table = rope_tables(length, HD)
    cos_query = cosine[None, :, None, None, :]
    sin_query = sine_table[None, :, None, None, :]
    cos_key = cosine[None, :, None, :]
    sin_key = sine_table[None, :, None, :]
    query = rotate(
        proj[..., :q_cols].reshape(seq_count, length, heads_k, group_size, HD), cos_query, sin_query
    ).astype(jnp.bfloat16)
    key_rot = rotate(
        proj[..., q_cols : q_cols + kv_cols].reshape(seq_count, length, heads_k, HD),
        cos_key,
        sin_key,
    ).astype(jnp.bfloat16)
    value_b = (
        proj[..., q_cols + kv_cols :].reshape(seq_count, length, heads_k, HD).astype(jnp.bfloat16)
    )
    d_out = d_ctx.reshape(seq_count, length, heads_k, group_size, HD).astype(jnp.bfloat16)
    score_scale = 1.0 / math.sqrt(HD)
    scores = contract("bqhgd,bkhd->bhgqk", query, key_rot) * score_scale
    positions = jnp.arange(length)
    causal = positions[:, None] >= positions[None, :]
    same_doc = documents[:, :, None] == documents[:, None, :]
    allowed = (causal[None] & same_doc)[:, None, None, :, :]
    exp_scores = jnp.where(allowed, jnp.exp(scores), 0.0)
    probs_f = exp_scores / jnp.sum(exp_scores, -1, keepdims=True)
    probs_b = probs_f.astype(jnp.bfloat16)
    context = contract("bhgqk,bkhd->bqhgd", probs_b, value_b).astype(jnp.bfloat16)
    d_probs = contract("bqhgd,bkhd->bhgqk", d_out, value_b)
    d_value = contract("bhgqk,bqhgd->bkhd", probs_b, d_out).astype(jnp.bfloat16)
    delta_sum = jnp.sum(probs_f * d_probs, -1, keepdims=True)
    d_scores = (probs_f * (d_probs - delta_sum) * score_scale).astype(jnp.bfloat16)
    d_query = contract("bhgqk,bkhd->bqhgd", d_scores, key_rot)
    d_key = contract("bhgqk,bqhgd->bkhd", d_scores, query)
    d_query = unrotate(d_query, cos_query, sin_query).astype(jnp.bfloat16)
    d_key = unrotate(d_key, cos_key, sin_key).astype(jnp.bfloat16)
    d_proj = jnp.concatenate(
        [
            d_query.reshape(seq_count, length, q_cols),
            d_key.reshape(seq_count, length, kv_cols),
            d_value.reshape(seq_count, length, kv_cols),
        ],
        -1,
    )
    return (d_proj, context.reshape(seq_count, length, q_cols))


def mix_three(center, from_low, from_high, c_low, c_high):
    return center + c_low * (from_low - center) + c_high * (from_high - center)


def body(hidden, cotangent, documents, q_weight, k_weight, v_weight, o_weight, edge_weight):
    full_hidden, full_cotan = (
        lax.all_gather(hidden, "tensor", axis=3, tiled=True),
        lax.all_gather(cotangent, "tensor", axis=3, tiled=True),
    )
    seq_count, length, model_width = full_hidden.shape[1:]
    token_rows = seq_count * length
    hidden_f = full_hidden[0].reshape(token_rows, model_width).astype(jnp.float32)
    normed = (
        hidden_f * lax.rsqrt(jnp.mean(hidden_f * hidden_f, -1, keepdims=True) + norm_eps)
    ).astype(jnp.bfloat16)
    cotan_rows = full_cotan[0].reshape(token_rows, model_width)
    q_cols = q_weight.shape[2]
    kv_cols = k_weight.shape[2]
    proj_cols = q_cols + 2 * kv_cols
    packed = jnp.concatenate([q_weight[0], k_weight[0], v_weight[0], o_weight[0]], 1).astype(
        jnp.bfloat16
    )
    block_rows = lax.all_gather(packed, "fsdp", axis=0, tiled=True)
    left = normed
    right = cotan_rows
    proj = jnp.dot(left, block_rows[:, :proj_cols], preferred_element_type=jnp.float32)
    d_ctx = jnp.dot(right, block_rows[:, proj_cols:], preferred_element_type=jnp.float32)
    d_proj, context = attention_grads(
        proj.reshape(seq_count, length, proj_cols),
        d_ctx.reshape(seq_count, length, q_cols),
        documents[0],
        q_cols // HD,
        kv_cols // HD,
    )
    d_proj = d_proj.reshape(token_rows, proj_cols)
    context = context.reshape(token_rows, q_cols)
    contract_rows = (((0,), (0,)), ((), ()))
    left = normed
    right = cotan_rows
    first_part = lax.dot_general(left, d_proj, contract_rows, preferred_element_type=jnp.float32)
    second_part = lax.dot_general(right, context, contract_rows, preferred_element_type=jnp.float32)
    gradients = lax.psum_scatter(
        jnp.concatenate([first_part, second_part], 1).astype(jnp.bfloat16),
        "fsdp",
        scatter_dimension=0,
        tiled=True,
    ).astype(jnp.float32)
    grad_q = gradients[None, :, :q_cols]
    grad_k = gradients[None, :, q_cols : q_cols + kv_cols]
    grad_v = gradients[None, :, q_cols + kv_cols : proj_cols]
    grad_o = gradients[None, :, proj_cols:]
    c_high = edge_weight[0]
    new_q = q_weight - learn_rate * grad_q
    new_k = k_weight - learn_rate * grad_k
    new_v = v_weight - learn_rate * grad_v
    new_o = o_weight - learn_rate * grad_o
    from_low = passed_along((new_q, new_k, new_v, new_o, edge_weight), "gossip", 1)
    from_high = passed_along((new_q, new_k, new_v, new_o), "gossip", -1)
    c_low = from_low[4][0]
    return (
        mix_three(new_q, from_low[0], from_high[0], c_low, c_high),
        mix_three(new_k, from_low[1], from_high[1], c_low, c_high),
        mix_three(new_v, from_low[2], from_high[2], c_low, c_high),
        mix_three(new_o, from_low[3], from_high[3], c_low, c_high),
    )


def solution(mesh):
    return jax.shard_map(
        body,
        mesh=mesh,
        in_specs=(
            P("gossip", "fsdp", None, "tensor"),
            P("gossip", "fsdp", None, "tensor"),
            P("gossip", "fsdp", None),
            P("gossip", "fsdp", "tensor"),
            P("gossip", "fsdp", "tensor"),
            P("gossip", "fsdp", "tensor"),
            P("gossip", "fsdp", "tensor"),
            P("gossip"),
        ),
        out_specs=(
            P("gossip", "fsdp", "tensor"),
            P("gossip", "fsdp", "tensor"),
            P("gossip", "fsdp", "tensor"),
            P("gossip", "fsdp", "tensor"),
        ),
        check_vma=False,
    )
```

profile of v0, /device:TPU:0, one launch (start us, length us, event | category | flops | bytes accessed | tf_op | source)
XLA Modules:
  0.0 878.4 jit_solution(919153522589254380)
XLA Ops:
  9.6 4.0 convert_bitcast_fusion
  17.9 28.8 %all-gather.4.cloned.1.call-done = bf16[1,2,256,4096]{3,2,1,0:T(8,128)(2,1)} async-done(((bf16[1,2,256,1024]{3,2,1,0:T(8,128)(2,1)}), bf16[1,2,256,4096]{3,2,1,0:T(8,128)(2,1)}) %all-gather.4.cloned.1.call-update) | async-done | bytes 4194320 | tf_op jit(solution)/shard_map/all_gather | solution.py:115
  50.2 3.4 fusion.1
  53.6 124.3 %all-gather.6.cloned.1.call-done = bf16[4096,1280]{1,0:T(8,128)(2,1)} async-done(((bf16[2048,1280]{1,0:T(8,128)(2,1)}), bf16[4096,1280]{1,0:T(8,128)(2,1)}) %all-gather.6.cloned.1.call-update) | async-done | bytes 10485776 | tf_op jit(solution)/shard_map/all_gather | solution.py:131
  177.9 7.3 fusion.2
  189.2 24.8 %all-gather.8.cloned.1.call-done = bf16[1,2,256,4096]{3,2,1,0:T(8,128)(2,1)} async-done(((bf16[1,2,256,1024]{3,2,1,0:T(8,128)(2,1)}), bf16[1,2,256,4096]{3,2,1,0:T(8,128)(2,1)}) %all-gather.8.cloned.1.call-update) | async-done | bytes 4194320 | tf_op jit(solution)/shard_map/all_gather | solution.py:116
  214.0 6.7 fusion.23
  230.9 5.0 fusion.3
  235.9 4.3 convolution_convert_fusion
  240.2 9.6 %pad_maximum_fusion = bf16[4096,1280]{0,1:T(8,128)(2,1)} fusion(bf16[4096,512]{0,1:T(8,128)(2,1)S(1)} %fusion.3, bf16[4096,768]{0,1:T(8,128)(2,1)S(1)} %convolution_convert_fusion), kind=kLoop, calls=%fused_computation | loop fusion | flops 20971520 | bytes 20971520 | tf_op jit(solution)/shard_map/concatenate | solution.py:151
  249.8 5.3 copy.49
  255.2 6.0 copy.52
  263.8 108.0 %reduce-scatter.2.cloned.1.call-done = bf16[2048,1280]{0,1:T(8,128)(2,1)} async-done(((bf16[4096,1280]{0,1:T(8,128)(2,1)}), bf16[2048,1280]{0,1:T(8,128)(2,1)}) %reduce-scatter.2.cloned.1.call-update) | async-done | bytes 5242896 | tf_op jit(solution)/shard_map/reduce_scatter | solution.py:150
  371.8 4.0 convert_element_type.107
  375.9 4.0 copy-done
  382.1 10.4 %fusion.6 = (f32[1,2048,512]{1,2,0:T(8,128)}, f32[1,2048,512]{1,2,0:T(8,128)}) fusion(f32[1,2048,512]{1,2,0:T(8,128)} %copy.52, f32[2048,1280]{0,1:T(8,128)} %copy-done, f32[1,2048,512]{1,2,0:T(8,128)S(1)} %copy-done.2), kind=kLoop, calls=%fused_computation.14 | loop fusion | flops 4194304 | bytes 25165824 | tf_op jit(solution)/shard_map/sub | solution.py:164
  398.3 210.9 %collective-permute-done = f32[1]{0:T(128)} collective-permute-done((f32[1]{0:T(128)}, f32[1]{0:T(128)}, u32[]{:S(2)}, u32[]{:S(2)}) %collective-permute-start) | collective-permute-done | bytes 36 | tf_op jit(solution)/shard_map/ppermute | solution.py:15
  609.3 3.8 collective-permute-start.2
  613.1 202.5 %collective-permute-done.3 = f32[1,2048,128]{1,2,0:T(8,128)S(1)} collective-permute-done((f32[1,2048,128]{1,2,0:T(8,128)S(1)}, f32[1,2048,128]{1,2,0:T(8,128)S(1)}, u32[]{:S(2)}, u32[]{:S(2)}) %collective-permute-start.3) | collective-permute-done | bytes 1048608 | tf_op jit(solution)/shard_map/ppermute | solution.py:15
  820.7 18.3 %collective-permute-done.4 = f32[1,2048,128]{1,2,0:T(8,128)} collective-permute-done((f32[1,2048,128]{1,2,0:T(8,128)S(1)}, f32[1,2048,128]{1,2,0:T(8,128)}, u32[]{:S(2)}, u32[]{:S(2)}) %collective-permute-start.4) | collective-permute-done | bytes 1048608 | tf_op jit(solution)/shard_map/ppermute | solution.py:15
  842.8 9.2 %multiply_add_fusion = f32[1,2048,512]{1,2,0:T(8,128)} fusion(f32[1,2048,512]{1,2,0:T(8,128)} %collective-permute-done.8, f32[1,2048,512]{1,2,0:T(8,128)} %get-tuple-element.12, f32[1,2048,512]{1,2,0:T(8,128)} %collective-permute-done.7, f32[]{:T(128)} %bitcast.169, f32[]{:T(128)} %bitcast.46), kind=kLoop, calls=%fused_computation.21 | loop fusion | flops 6291456 | bytes 16777224 | tf_op jit(solution)/shard_map/add | solution.py:110
  852.0 5.3 copy.56
  857.3 9.2 %multiply_add_fusion.1 = f32[1,2048,512]{1,2,0:T(8,128)} fusion(f32[1,2048,512]{1,2,0:T(8,128)} %collective-permute-done.2, f32[1,2048,512]{1,2,0:T(8,128)} %get-tuple-element.13, f32[1,2048,512]{1,2,0:T(8,128)} %collective-permute-done.1, f32[]{:T(128)} %bitcast.167, f32[]{:T(128)} %bitcast.46), kind=kLoop, calls=%fused_computation.22 | loop fusion | flops 6291456 | bytes 16777224 | tf_op jit(solution)/shard_map/add | solution.py:110
  866.6 5.3 copy.53
  (82 shorter events, 43.1 us)
Async XLA Ops:
  7.2 39.6 %all-gather.4.cloned.1.call-start = ((), (), s32[]{:S(2)}) async-start(), calls=%async_computation.1 | async-start | bytes 5242880 | tf_op jit(solution)/shard_map/all_gather | solution.py:115
  7.9 170.0 %all-gather.6.cloned.1.call-start = ((), (), s32[]{:S(2)}) async-start(), calls=%async_computation.2 | async-start | bytes 15728640 | tf_op jit(solution)/shard_map/all_gather | solution.py:131
  16.4 197.5 %all-gather.8.cloned.1.call-start = ((), (), s32[]{:S(2)}) async-start(), calls=%async_computation.3 | async-start | bytes 5242880 | tf_op jit(solution)/shard_map/all_gather | solution.py:116
  17.2 354.7 %reduce-scatter.2.cloned.1.call-start = ((), (), s32[]{:S(2)}) async-start(), calls=%async_computation.4 | async-start | bytes 15728640 | tf_op jit(solution)/shard_map/reduce_scatter | solution.py:150
  46.8 3.4 copy-start.1
  185.2 1.1 copy-start.9
  214.0 7.9 copy-start.8
  230.9 5.0 copy-start.3
  255.2 6.0 copy-start.4
  255.2 7.3 copy-start.5
  371.8 8.1 copy-start.6
  371.8 8.1 copy-start.7
  375.9 4.0 copy-start
  379.9 2.2 copy-start.2
  380.3 229.0 %collective-permute-start.5 = (f32[1,2048,128]{1,2,0:T(8,128)S(1)}, f32[1,2048,128]{1,2,0:T(8,128)}, u32[]{:S(2)}, u32[]{:S(2)}) collective-permute-start(f32[1,2048,128]{1,2,0:T(8,128)S(1)} %get-tuple-element.14), channel_id=1, source_target_pairs={{0,8},{8,16},{16,24},{24,0},{1,9},{9,17},{17,25},{25,1},{2,10},{10... | collective-permute-start | bytes 3145736 | tf_op jit(solution)/shard_map/ppermute | solution.py:15
  392.5 450.3 %collective-permute-start.7 = (f32[1,2048,512]{1,2,0:T(8,128)}, f32[1,2048,512]{1,2,0:T(8,128)}, u32[]{:S(2)}, u32[]{:S(2)}) collective-permute-start(f32[1,2048,512]{1,2,0:T(8,128)} %get-tuple-element.12), channel_id=1, source_target_pairs={{0,8},{8,16},{16,24},{24,0},{1,9},{9,17},{17,25},{25,1},{2,10},{10... | collective-permute-start | bytes 12582920 | tf_op jit(solution)/shard_map/ppermute | solution.py:15
  394.0 448.8 %collective-permute-start.8 = (f32[1,2048,512]{1,2,0:T(8,128)}, f32[1,2048,512]{1,2,0:T(8,128)}, u32[]{:S(2)}, u32[]{:S(2)}) collective-permute-start(f32[1,2048,512]{1,2,0:T(8,128)} %get-tuple-element.12), channel_id=1, source_target_pairs={{0,24},{8,0},{16,8},{24,16},{1,25},{9,1},{17,9},{25,17},{2,26},{10... | collective-permute-start | bytes 12582920 | tf_op jit(solution)/shard_map/ppermute | solution.py:15
  396.3 216.8 %collective-permute-start.6 = (f32[1,2048,128]{1,2,0:T(8,128)S(1)}, f32[1,2048,128]{1,2,0:T(8,128)S(1)}, u32[]{:S(2)}, u32[]{:S(2)}) collective-permute-start(f32[1,2048,128]{1,2,0:T(8,128)S(1)} %get-tuple-element.14), channel_id=1, source_target_pairs={{0,24},{8,0},{16,8},{24,16},{1,25},{9,1},{17,9},{25,17},{2,26},{10... | collective-permute-start | bytes 3145736 | tf_op jit(solution)/shard_map/ppermute | solution.py:15
  397.8 211.4 %collective-permute-start = (f32[1]{0:T(128)}, f32[1]{0:T(128)}, u32[]{:S(2)}, u32[]{:S(2)}) collective-permute-start(f32[1]{0:T(128)} %param.15), channel_id=1, source_target_pairs={{0,8},{8,16},{16,24},{24,0},{1,9},{9,17},{17,25},{25,1},{2,10},{10... | collective-permute-start | bytes 20 | tf_op jit(solution)/shard_map/ppermute | solution.py:15
  609.3 248.1 %collective-permute-start.1 = (f32[1,2048,512]{1,2,0:T(8,128)}, f32[1,2048,512]{1,2,0:T(8,128)}, u32[]{:S(2)}, u32[]{:S(2)}) collective-permute-start(f32[1,2048,512]{1,2,0:T(8,128)} %get-tuple-element.13), channel_id=1, source_target_pairs={{0,8},{8,16},{16,24},{24,0},{1,9},{9,17},{17,25},{25,1},{2,10},{10... | collective-permute-start | bytes 12582920 | tf_op jit(solution)/shard_map/ppermute | solution.py:15
  609.3 248.1 %collective-permute-start.2 = (f32[1,2048,512]{1,2,0:T(8,128)}, f32[1,2048,512]{1,2,0:T(8,128)}, u32[]{:S(2)}, u32[]{:S(2)}) collective-permute-start(f32[1,2048,512]{1,2,0:T(8,128)} %get-tuple-element.13), channel_id=1, source_target_pairs={{0,24},{8,0},{16,8},{24,16},{1,25},{9,1},{17,9},{25,17},{2,26},{10... | collective-permute-start | bytes 12582920 | tf_op jit(solution)/shard_map/ppermute | solution.py:15
  613.1 202.5 %collective-permute-start.3 = (f32[1,2048,128]{1,2,0:T(8,128)S(1)}, f32[1,2048,128]{1,2,0:T(8,128)S(1)}, u32[]{:S(2)}, u32[]{:S(2)}) collective-permute-start(f32[1,2048,128]{1,2,0:T(8,128)S(1)} %get-tuple-element.15), channel_id=1, source_target_pairs={{0,8},{8,16},{16,24},{24,0},{1,9},{9,17},{17,25},{25,1},{2,10},{10... | collective-permute-start | bytes 3145736 | tf_op jit(solution)/shard_map/ppermute | solution.py:15
  815.6 1.0 copy-start.10
  816.6 22.5 %collective-permute-start.4 = (f32[1,2048,128]{1,2,0:T(8,128)S(1)}, f32[1,2048,128]{1,2,0:T(8,128)}, u32[]{:S(2)}, u32[]{:S(2)}) collective-permute-start(f32[1,2048,128]{1,2,0:T(8,128)S(1)} %get-tuple-element.15), channel_id=1, source_target_pairs={{0,24},{8,0},{16,8},{24,16},{1,25},{9,1},{17,9},{25,17},{2,26},{10... | collective-permute-start | bytes 3145736 | tf_op jit(solution)/shard_map/ppermute | solution.py:15
  (1 other events, 0.9 us)
Sparse Core Ops, SparseCore 0:
  9.6 37.1 all-gather.3
  48.3 129.5 all-gather.5
  179.4 34.4 all-gather.7
  249.9 121.8 reduce-scatter.1
where the time goes:
time: 879 us; the launch traced here: 878 us
  waiting for transfers between devices  719 us (82%)
  other arithmetic  65.3 us (7%)
  local copies, waits for them, and re-layouts  38.7 us (4%)
  matrix products  29.3 us (3%)
  between operations  14.7 us (2%)
  starting transfers between devices  11.4 us (1%)
    ppermute x9, waiting for transfers between devices, passed_along(): lax.ppermute(shard, axis, [(i, (i + by) % count) for i in range(count)])  432 us
    all_gather x1, waiting for transfers between devices, body(): block_rows = lax.all_gather(packed, 'fsdp', axis=0, tiled=True)  124 us
    reduce_scatter x1, waiting for transfers between devices, body(): lax.psum_scatter(jnp.concatenate([first_part, second_part], 1).astype(jnp...  108 us
    unnamed x34, local copies, waits for them, and re-layouts  33.9 us
    all_gather x1, waiting for transfers between devices, body(): lax.all_gather(hidden, 'tensor', axis=3, tiled=True)  28.8 us
    all_gather x1, waiting for transfers between devices, body(): lax.all_gather(cotangent, 'tensor', axis=3, tiled=True)  24.8 us
    add x4, other arithmetic, mix_three(): return center + c_low * (from_low - center) + c_high * (from_high - center)  23 us
  transfers between devices with their start and end apart: 13, of which 7 were waited for; matrix products, arithmetic and copies ran while one was open for 8% of the time, Pallas kernels for 0%

commit v1 on v0

--- a/solution.py
+++ b/solution.py
@@ -3,6 +3,7 @@
 import jax.numpy as jnp
 from jax import lax
 from jax.sharding import PartitionSpec as P
+from jax.lax import axis_index, axis_size, ppermute
 
 HD = 128
 rope_theta = 500000.0
@@ -111,9 +112,23 @@
 
 
 def body(hidden, cotangent, documents, q_weight, k_weight, v_weight, o_weight, edge_weight):
+
+    def _take_spot(block_in):
+        taken_in, opened, shaped = (axis_size("tensor"), axis_index("tensor"), block_in.shape[3])
+        current_arr, found_now = (block_in, 1)
+        while found_now < taken_in:
+            seen = []
+            for p in range(taken_in):
+                seen.append((p, (p - found_now) % taken_in))
+            current_arr = jnp.concatenate(
+                [current_arr, ppermute(current_arr, "tensor", perm=seen)], 3
+            )
+            found_now = 2 * found_now
+        return jnp.roll(current_arr, opened * shaped, 3)
+
     full_hidden, full_cotan = (
         lax.all_gather(hidden, "tensor", axis=3, tiled=True),
-        lax.all_gather(cotangent, "tensor", axis=3, tiled=True),
+        _take_spot(cotangent),
     )
     seq_count, length, model_width = full_hidden.shape[1:]
     token_rows = seq_count * length

time: 879 us -> 873 us (level)
  waiting for transfers between devices: 719 us -> 693 us
  local copies, waits for them, and re-layouts: 38.7 us -> 55.4 us
    ppermute x0 -> x2, waiting for transfers between devices: none -> 81.7 us  [_take_spot(): ppermute(current_arr, 'tensor', perm=seen)]
    all_gather x1, waiting for transfers between devices: 124 us -> 71.7 us  [body(): block_rows = lax.all_gather(packed, 'fsdp', axis=0, tiled=True)]
    all_gather x1, waiting for transfers between devices: 28.8 us -> 0.01 us  [body(): lax.all_gather(hidden, 'tensor', axis=3, tiled=True)]
    all_gather x1 -> x0, waiting for transfers between devices: 24.8 us -> none  [body(): lax.all_gather(cotangent, 'tensor', axis=3, tiled=True)]
    dot_general x0 -> x2, local copies, waits for them, and re-layouts: none -> 10.9 us  [body(): jnp.dot(right, block_rows[:, proj_cols:], preferred_element_type=jnp.floa...]
    unnamed x34 -> x41, local copies, waits for them, and re-layouts: 33.9 us -> 38.5 us
  transfers between devices with their start and end apart: 13 -> 14, of which waited for: 7 -> 7; matrix products, arithmetic and copies ran while one was open for 8% -> 8% of each run, Pallas kernels for 0% -> 0%
where the time goes in v1:
time: 873 us; the launch traced here: 872 us
  waiting for transfers between devices  693 us (79%)
  other arithmetic  66.8 us (8%)
  local copies, waits for them, and re-layouts  55.4 us (6%)
  matrix products  27 us (3%)
  starting transfers between devices  15.4 us (2%)
  between operations  14.7 us (2%)
    ppermute x9, waiting for transfers between devices, passed_along(): lax.ppermute(shard, axis, [(i, (i + by) % count) for i in range(count)])  430 us
    reduce_scatter x1, waiting for transfers between devices, body(): lax.psum_scatter(jnp.concatenate([first_part, second_part], 1).astype(jnp...  108 us
    ppermute x2, waiting for transfers between devices, _take_spot(): ppermute(current_arr, 'tensor', perm=seen)  81.7 us
    all_gather x1, waiting for transfers between devices, body(): block_rows = lax.all_gather(packed, 'fsdp', axis=0, tiled=True)  71.7 us
    unnamed x41, local copies, waits for them, and re-layouts  38.5 us
    add x4, other arithmetic, mix_three(): return center + c_low * (from_low - center) + c_high * (from_high - center)  23 us
  transfers between devices with their start and end apart: 14, of which 7 were waited for; matrix products, arithmetic and copies ran while one was open for 8% of the time, Pallas kernels for 0%

profile of v1, /device:TPU:0, one launch (start us, length us, event | category | flops | bytes accessed | tf_op | source)
XLA Modules:
  0.0 872.0 jit_solution(9807207163967400576)
XLA Ops:
  9.6 4.0 convert_bitcast_fusion
  20.1 34.1 %collective-permute-done = bf16[1,2,256,1024]{3,2,1,0:T(8,128)(2,1)S(1)} collective-permute-done((bf16[1,2,256,1024]{3,2,1,0:T(8,128)(2,1)S(1)}, bf16[1,2,256,1024]{3,2,1,0:T(8,128)(2,1)S(1)}, u32[]{:S(2)}, u32[]{:S(2)}) %collective-permute-start) | collective-permute-done | bytes 1048608 | tf_op jit(solution)/shard_map/ppermute | solution.py:124
  56.9 47.6 %collective-permute-done.1 = bf16[1,2,256,2048]{3,2,1,0:T(8,128)(2,1)} collective-permute-done((bf16[1,2,256,2048]{3,2,1,0:T(8,128)(2,1)}, bf16[1,2,256,2048]{3,2,1,0:T(8,128)(2,1)}, u32[]{:S(2)}, u32[]{:S(2)}) %collective-permute-start.1) | collective-permute-done | bytes 2097184 | tf_op jit(solution)/shard_map/ppermute | solution.py:124
  117.3 71.7 %all-gather.5.cloned.1.call-done = bf16[4096,1280]{1,0:T(8,128)(2,1)} async-done(((bf16[2048,1280]{1,0:T(8,128)(2,1)}), bf16[4096,1280]{1,0:T(8,128)(2,1)}) %all-gather.5.cloned.1.call-update) | async-done | bytes 10485776 | tf_op jit(solution)/shard_map/all_gather | solution.py:146
  189.0 7.1 fusion.2
  197.4 4.5 slice_bitcast_fusion.2
  201.9 6.4 copy.73
  210.8 4.5 fusion.18
  224.5 4.7 convolution_convert_fusion.1
  229.2 4.5 convolution_convert_fusion
  233.7 9.6 %pad_maximum_fusion = bf16[4096,1280]{0,1:T(8,128)(2,1)} fusion(bf16[4096,512]{0,1:T(8,128)(2,1)S(1)} %convolution_convert_fusion.1, bf16[4096,768]{0,1:T(8,128)(2,1)S(1)} %convolution_convert_fusion), kind=kLoop, calls=%fused_computation | loop fusion | flops 20971520 | bytes 20971520 | tf_op jit(solution)/shard_map/concatenate | solution.py:166
  243.4 5.3 copy.49
  248.7 6.0 copy.52
  257.4 108.0 %reduce-scatter.2.cloned.1.call-done = bf16[2048,1280]{0,1:T(8,128)(2,1)} async-done(((bf16[4096,1280]{0,1:T(8,128)(2,1)}), bf16[2048,1280]{0,1:T(8,128)(2,1)}) %reduce-scatter.2.cloned.1.call-update) | async-done | bytes 5242896 | tf_op jit(solution)/shard_map/reduce_scatter | solution.py:165
  365.4 4.0 convert_element_type.96
  369.5 4.0 copy-done
  375.7 10.4 %fusion.5 = (f32[1,2048,512]{1,2,0:T(8,128)}, f32[1,2048,512]{1,2,0:T(8,128)}) fusion(f32[1,2048,512]{1,2,0:T(8,128)} %copy.52, f32[2048,1280]{0,1:T(8,128)} %copy-done, f32[1,2048,512]{1,2,0:T(8,128)S(1)} %copy-done.2), kind=kLoop, calls=%fused_computation.13 | loop fusion | flops 4194304 | bytes 25165824 | tf_op jit(solution)/shard_map/sub | solution.py:179
  393.2 209.7 %collective-permute-done.2 = f32[1]{0:T(128)} collective-permute-done((f32[1]{0:T(128)}, f32[1]{0:T(128)}, u32[]{:S(2)}, u32[]{:S(2)}) %collective-permute-start.2) | collective-permute-done | bytes 36 | tf_op jit(solution)/shard_map/ppermute | solution.py:16
  606.7 202.5 %collective-permute-done.5 = f32[1,2048,128]{1,2,0:T(8,128)S(1)} collective-permute-done((f32[1,2048,128]{1,2,0:T(8,128)S(1)}, f32[1,2048,128]{1,2,0:T(8,128)S(1)}, u32[]{:S(2)}, u32[]{:S(2)}) %collective-permute-start.5) | collective-permute-done | bytes 1048608 | tf_op jit(solution)/shard_map/ppermute | solution.py:16
  814.3 18.3 %collective-permute-done.6 = f32[1,2048,128]{1,2,0:T(8,128)} collective-permute-done((f32[1,2048,128]{1,2,0:T(8,128)S(1)}, f32[1,2048,128]{1,2,0:T(8,128)}, u32[]{:S(2)}, u32[]{:S(2)}) %collective-permute-start.6) | collective-permute-done | bytes 1048608 | tf_op jit(solution)/shard_map/ppermute | solution.py:16
  836.4 9.2 %multiply_add_fusion = f32[1,2048,512]{1,2,0:T(8,128)} fusion(f32[1,2048,512]{1,2,0:T(8,128)} %collective-permute-done.10, f32[1,2048,512]{1,2,0:T(8,128)} %get-tuple-element.12, f32[1,2048,512]{1,2,0:T(8,128)} %collective-permute-done.9, f32[]{:T(128)} %bitcast.178, f32[]{:T(128)} %bitcast.50), kind=kLoop, calls=%fused_computation.21 | loop fusion | flops 6291456 | bytes 16777224 | tf_op jit(solution)/shard_map/add | solution.py:111
  845.6 5.3 copy.56
  850.9 9.2 %multiply_add_fusion.1 = f32[1,2048,512]{1,2,0:T(8,128)} fusion(f32[1,2048,512]{1,2,0:T(8,128)} %collective-permute-done.4, f32[1,2048,512]{1,2,0:T(8,128)} %get-tuple-element.13, f32[1,2048,512]{1,2,0:T(8,128)} %collective-permute-done.3, f32[]{:T(128)} %bitcast.176, f32[]{:T(128)} %bitcast.50), kind=kLoop, calls=%fused_computation.22 | loop fusion | flops 6291456 | bytes 16777224 | tf_op jit(solution)/shard_map/add | solution.py:111
  860.2 5.3 copy.53
  (94 shorter events, 61.0 us)
Async XLA Ops:
  7.2 103.3 %all-gather.3.cloned.1.call-start = ((), (), s32[]{:S(2)}) async-start(), calls=%async_computation.1 | async-start | bytes 5242880 | tf_op jit(solution)/shard_map/all_gather | solution.py:130
  7.9 181.1 %all-gather.5.cloned.1.call-start = ((), (), s32[]{:S(2)}) async-start(), calls=%async_computation.2 | async-start | bytes 15728640 | tf_op jit(solution)/shard_map/all_gather | solution.py:146
  16.4 39.8 %copy-start.12 = (s32[1,2,256]{2,1,0:T(2,128)S(1)}, s32[1,2,256]{2,1,0:T(2,128)}, u32[]{:S(2)}) copy-start(s32[1,2,256]{2,1,0:T(2,128)} %param.10) | copy-start | bytes 6148
  16.4 349.0 %reduce-scatter.2.cloned.1.call-start = ((), (), s32[]{:S(2)}) async-start(), calls=%async_computation.3 | async-start | bytes 15728640 | tf_op jit(solution)/shard_map/reduce_scatter | solution.py:165
  17.6 36.6 %collective-permute-start = (bf16[1,2,256,1024]{3,2,1,0:T(8,128)(2,1)S(1)}, bf16[1,2,256,1024]{3,2,1,0:T(8,128)(2,1)S(1)}, u32[]{:S(2)}, u32[]{:S(2)}) collective-permute-start(bf16[1,2,256,1024]{3,2,1,0:T(8,128)(2,1)S(1)} %copy-done.3), channel_id=1, source_target_pairs={{0,3},{1,0},{2,1},{3,2},{4,7},{5,4},{6,5},{7,6},{8,11},{9,8},{10,9... | collective-permute-start | bytes 3145736 | tf_op jit(solution)/shard_map/ppermute | solution.py:124
  55.7 48.8 %collective-permute-start.1 = (bf16[1,2,256,2048]{3,2,1,0:T(8,128)(2,1)}, bf16[1,2,256,2048]{3,2,1,0:T(8,128)(2,1)}, u32[]{:S(2)}, u32[]{:S(2)}) collective-permute-start(bf16[1,2,256,2048]{3,2,1,0:T(8,128)(2,1)} %pad_maximum_fusion.2), channel_id=1, source_target_pairs={{0,2},{1,3},{2,0},{3,1},{4,6},{5,7},{6,4},{7,5},{8,10},{9,11},{10,... | collective-permute-start | bytes 6291464 | tf_op jit(solution)/shard_map/ppermute | solution.py:124
  110.4 3.4 copy-start.1
  208.6 2.2 copy-start.7
  224.5 4.7 copy-start.4
  248.7 6.0 copy-start.5
  248.7 7.3 copy-start.6
  365.4 8.1 copy-start.8
  365.4 8.1 copy-start.9
  369.4 4.0 copy-start
  373.5 2.2 copy-start.2
  373.9 229.0 %collective-permute-start.7 = (f32[1,2048,128]{1,2,0:T(8,128)S(1)}, f32[1,2048,128]{1,2,0:T(8,128)}, u32[]{:S(2)}, u32[]{:S(2)}) collective-permute-start(f32[1,2048,128]{1,2,0:T(8,128)S(1)} %get-tuple-element.14), channel_id=1, source_target_pairs={{0,8},{8,16},{16,24},{24,0},{1,9},{9,17},{17,25},{25,1},{2,10},{10... | collective-permute-start | bytes 3145736 | tf_op jit(solution)/shard_map/ppermute | solution.py:16
  386.1 450.3 %collective-permute-start.10 = (f32[1,2048,512]{1,2,0:T(8,128)}, f32[1,2048,512]{1,2,0:T(8,128)}, u32[]{:S(2)}, u32[]{:S(2)}) collective-permute-start(f32[1,2048,512]{1,2,0:T(8,128)} %get-tuple-element.12), channel_id=1, source_target_pairs={{0,24},{8,0},{16,8},{24,16},{1,25},{9,1},{17,9},{25,17},{2,26},{10... | collective-permute-start | bytes 12582920 | tf_op jit(solution)/shard_map/ppermute | solution.py:16
  389.4 447.0 %collective-permute-start.9 = (f32[1,2048,512]{1,2,0:T(8,128)}, f32[1,2048,512]{1,2,0:T(8,128)}, u32[]{:S(2)}, u32[]{:S(2)}) collective-permute-start(f32[1,2048,512]{1,2,0:T(8,128)} %get-tuple-element.12), channel_id=1, source_target_pairs={{0,8},{8,16},{16,24},{24,0},{1,9},{9,17},{17,25},{25,1},{2,10},{10... | collective-permute-start | bytes 12582920 | tf_op jit(solution)/shard_map/ppermute | solution.py:16
  389.4 217.3 %collective-permute-start.8 = (f32[1,2048,128]{1,2,0:T(8,128)S(1)}, f32[1,2048,128]{1,2,0:T(8,128)S(1)}, u32[]{:S(2)}, u32[]{:S(2)}) collective-permute-start(f32[1,2048,128]{1,2,0:T(8,128)S(1)} %get-tuple-element.14), channel_id=1, source_target_pairs={{0,24},{8,0},{16,8},{24,16},{1,25},{9,1},{17,9},{25,17},{2,26},{10... | collective-permute-start | bytes 3145736 | tf_op jit(solution)/shard_map/ppermute | solution.py:16
  393.2 209.7 %collective-permute-start.2 = (f32[1]{0:T(128)}, f32[1]{0:T(128)}, u32[]{:S(2)}, u32[]{:S(2)}) collective-permute-start(f32[1]{0:T(128)} %param.15), channel_id=1, source_target_pairs={{0,8},{8,16},{16,24},{24,0},{1,9},{9,17},{17,25},{25,1},{2,10},{10... | collective-permute-start | bytes 20 | tf_op jit(solution)/shard_map/ppermute | solution.py:16
  602.9 248.1 %collective-permute-start.3 = (f32[1,2048,512]{1,2,0:T(8,128)}, f32[1,2048,512]{1,2,0:T(8,128)}, u32[]{:S(2)}, u32[]{:S(2)}) collective-permute-start(f32[1,2048,512]{1,2,0:T(8,128)} %get-tuple-element.13), channel_id=1, source_target_pairs={{0,8},{8,16},{16,24},{24,0},{1,9},{9,17},{17,25},{25,1},{2,10},{10... | collective-permute-start | bytes 12582920 | tf_op jit(solution)/shard_map/ppermute | solution.py:16
  602.9 248.1 %collective-permute-start.4 = (f32[1,2048,512]{1,2,0:T(8,128)}, f32[1,2048,512]{1,2,0:T(8,128)}, u32[]{:S(2)}, u32[]{:S(2)}) collective-permute-start(f32[1,2048,512]{1,2,0:T(8,128)} %get-tuple-element.13), channel_id=1, source_target_pairs={{0,24},{8,0},{16,8},{24,16},{1,25},{9,1},{17,9},{25,17},{2,26},{10... | collective-permute-start | bytes 12582920 | tf_op jit(solution)/shard_map/ppermute | solution.py:16
  606.7 202.5 %collective-permute-start.5 = (f32[1,2048,128]{1,2,0:T(8,128)S(1)}, f32[1,2048,128]{1,2,0:T(8,128)S(1)}, u32[]{:S(2)}, u32[]{:S(2)}) collective-permute-start(f32[1,2048,128]{1,2,0:T(8,128)S(1)} %get-tuple-element.15), channel_id=1, source_target_pairs={{0,8},{8,16},{16,24},{24,0},{1,9},{9,17},{17,25},{25,1},{2,10},{10... | collective-permute-start | bytes 3145736 | tf_op jit(solution)/shard_map/ppermute | solution.py:16
  810.2 22.5 %collective-permute-start.6 = (f32[1,2048,128]{1,2,0:T(8,128)S(1)}, f32[1,2048,128]{1,2,0:T(8,128)}, u32[]{:S(2)}, u32[]{:S(2)}) collective-permute-start(f32[1,2048,128]{1,2,0:T(8,128)S(1)} %get-tuple-element.15), channel_id=1, source_target_pairs={{0,24},{8,0},{16,8},{24,16},{1,25},{9,1},{17,9},{25,17},{2,26},{10... | collective-permute-start | bytes 3145736 | tf_op jit(solution)/shard_map/ppermute | solution.py:16
  (3 other events, 3.4 us)
Sparse Core Ops, SparseCore 0:
  9.6 47.9 all-gather.2
  59.1 129.9 all-gather.4
  243.5 121.8 reduce-scatter.1
